TPU v7x, 256 devices: a whole 4x4x8 slice. The times are simulated.
256 devices in a mesh: patch: 32 (over y, z), req: 4 (over x), owner: 2 (over core).
Axes of the slice: x: 4, y: 4, z: 8, core: 2. Of those that a mesh axis runs over, the one named last changes fastest.
Arguments:
- latents: bfloat16 [8, 256, 256, 320], P('req', 'patch', 'owner'), may hold values from -24 to 24
- timestep_embedding: bfloat16 [8, 1280], P('req'), may hold values from -6 to 6
- embedding_weight: bfloat16 [1280, 320], replicated, may hold values from -0.15625 to 0.15625
- group_norm_gain: float32 [2, 320], replicated, may hold values from 0.25 to 1.75
- group_norm_shift: float32 [2, 320], replicated, may hold values from -3 to 3
- kernel_weight: bfloat16 [2, 9, 320, 320], replicated, may hold values from -0.109375 to 0.109375
- plugin_reduce_library: bfloat16 [8, 2, 184320], P(('req', 'owner'), None, 'patch'), may hold values from -0.109375 to 0.109375
- plugin_expand_library: bfloat16 [8, 2, 20480], P(('req', 'owner'), None, 'patch'), may hold values from -0.75 to 0.75
- image_adapter: int32 [8, 1], P('req'), may hold values from 0 to 7
- adapter_bank_row: int32 [8], replicated, may hold values from 0 to 7, each once
Outputs:
- result: bfloat16 [8, 256, 256, 320], P('req', 'patch', 'owner')
Inputs may be any that keep to these rules, and one draw needn't show every extreme that they name: `image_adapter`: each image names one adapter; every adapter is named by some image. A permutation: adapter a is stored in bank row adapter_bank_row[a].
All inputs are finite; a program needn't handle non-finite values.
Results may differ from a plain program's by a relative error of at most 0.0055.
Values may be sent and summed in bfloat16 or wider, within the bound.
A program may use at most 128 MiB of HBM per device.

v0:
```python
import jax
import jax.numpy as jnp
from jax import lax
from jax.sharding import PartitionSpec as P

GROUPS = 32


def padded_2(block, sides, width):
    for axis, dim in sides:
        count = lax.axis_size(axis)
        forward = [(i, i + 1) for i in range(count - 1)]
        backward = [(target, source) for source, target in forward]
        low = lax.ppermute(
            lax.slice_in_dim(block, block.shape[dim] - width, None, axis=dim), axis, forward
        )
        high = lax.ppermute(lax.slice_in_dim(block, 0, width, axis=dim), axis, backward)
        block = jnp.concatenate([low, block, high], axis=dim)
    return block


def group_act(values, gain, shift):
    images, rows, columns, chans = values.shape
    grouped = values.reshape(images, rows, columns, GROUPS, chans // GROUPS)
    count = rows * columns * (chans // GROUPS) * lax.axis_size("patch") * lax.axis_size("owner")
    total = lax.psum(jnp.sum(grouped, axis=(1, 2, 4)), ("patch", "owner"))
    mean = total / count
    centered = grouped - mean[:, None, None, :, None]
    spread = lax.psum(jnp.sum(centered * centered, axis=(1, 2, 4)), ("patch", "owner"))
    var = spread / count
    normed = (centered / jnp.sqrt(var + 1e-05)[:, None, None, :, None]).reshape(values.shape)
    return jax.nn.silu(normed * gain + shift).astype(jnp.bfloat16)


def block_conv(act, kernel, reducing_filter, expanding_linear_map):
    images, rows, columns, chans = act.shape
    outward = kernel.shape[2]
    padded = padded_2(act, (("patch", 1), ("owner", 2)), 1)
    joined = jnp.concatenate(
        [jnp.broadcast_to(kernel[None], (images,) + kernel.shape), reducing_filter], axis=3
    )
    accum = jnp.zeros((images, rows, columns, joined.shape[3]), jnp.float32)
    for tap in range(9):
        row_off, col_off = divmod(tap, 3)
        window = padded[:, row_off : row_off + rows, col_off : col_off + columns, :]
        accum = accum + jnp.einsum(
            "bhwc,bcd->bhwd", window, joined[:, tap], preferred_element_type=jnp.float32
        )
    lowpart = accum[..., outward:].astype(jnp.bfloat16)
    return accum[..., :outward] + jnp.einsum(
        "bhwr,brd->bhwd", lowpart, expanding_linear_map, preferred_element_type=jnp.float32
    )


def local(
    latents,
    timestep_embedding,
    embedding_weight,
    group_norm_gain,
    group_norm_shift,
    kernel_weight,
    plugin_reduce_library,
    plugin_expand_library,
    image_adapter,
    adapter_bank_row,
):
    images, rows, columns, chans = latents.shape
    wanted = image_adapter[:, 0]
    table = jnp.arange(adapter_bank_row.shape[0], dtype=jnp.int32)
    slots = jnp.sum(
        jnp.where(wanted[:, None] == table[None, :], adapter_bank_row[None, :], 0), axis=1
    )
    full_down, full_up = (
        lax.all_gather(plugin_reduce_library, "patch", axis=2, tiled=True),
        lax.all_gather(plugin_expand_library, "patch", axis=2, tiled=True),
    )
    pieces = (
        lax.all_gather(full_down, ("req", "owner"), axis=0, tiled=True),
        lax.all_gather(full_up, ("req", "owner"), axis=0, tiled=True),
    )
    count = pieces[0].shape[0]
    match = (slots[:, None] == jnp.arange(count, dtype=jnp.int32)[None, :]).astype(jnp.bfloat16)
    first = jnp.einsum("ik,kjs->ijs", match, pieces[0], preferred_element_type=jnp.float32)
    second = jnp.einsum("ik,kjs->ijs", match, pieces[1], preferred_element_type=jnp.float32)
    down_sel = first.astype(jnp.bfloat16)
    up_sel = second.astype(jnp.bfloat16)
    rank = up_sel.shape[2] // chans
    down_all = down_sel.reshape(images, 2, 9, chans, rank)
    up_all = up_sel.reshape(images, 2, rank, chans)
    temb = jax.nn.silu(timestep_embedding.astype(jnp.float32)).astype(jnp.bfloat16)
    proj = jnp.dot(temb, embedding_weight, preferred_element_type=jnp.float32)
    source = latents.astype(jnp.float32)
    act1 = group_act(source, group_norm_gain[0], group_norm_shift[0])
    hidden1 = (
        block_conv(act1, kernel_weight[0], down_all[:, 0], up_all[:, 0]) + proj[:, None, None, :]
    ).astype(jnp.bfloat16)
    act2 = group_act(hidden1.astype(jnp.float32), group_norm_gain[1], group_norm_shift[1])
    result = source + block_conv(act2, kernel_weight[1], down_all[:, 1], up_all[:, 1])
    return result.astype(jnp.bfloat16)


def solution(mesh):
    in_specs = (
        P("req", "patch", "owner", None),
        P("req", None),
        P(),
        P(),
        P(),
        P(),
        P(("req", "owner"), None, "patch"),
        P(("req", "owner"), None, "patch"),
        P("req", None),
        P(),
    )
    out_specs = P("req", "patch", "owner", None)
    return jax.shard_map(local, mesh=mesh, in_specs=in_specs, out_specs=out_specs, check_vma=False)
```

profile of v0, /device:TPU:1, one launch (start us, length us, event | category | flops | bytes accessed | tf_op | source)
XLA Modules:
  0.0 778.4 jit_solution(10491722644223189108)
XLA Ops:
  6.6 47.2 %all_gather.12 = bf16[1,2,184320]{2,1,0:T(2,128)(2,1)} all-gather(bf16[1,2,5760]{2,1,0:T(2,128)(2,1)} %param.16), channel_id=1, replica_groups=mesh['patch'=32,'req'=4,'owner'=2] {'patch'}, dimensions={2}, use_global_device_ids=true | all-gather | bytes 760320 | tf_op jit(solution)/shard_map/all_gather | solution.py:74
  55.6 135.6 %psum.28 = f32[2,32]{1,0:T(2,128)S(1)} all-reduce(f32[2,32]{1,0:T(2,128)S(1)} %reduce_sum.59), channel_id=1, replica_groups=mesh['patch'=32,'req'=4,'owner'=2] {'patch','owner'}, use_global_device_ids=true, to_apply=%region_2.3 | all-reduce | flops 64 | bytes 512 | tf_op jit(solution)/shard_map/psum | solution.py:26
  192.2 124.0 %psum.29 = f32[2,32]{1,0:T(2,128)S(1)} all-reduce(f32[2,32]{1,0:T(2,128)S(1)} %reduce_sum.62), channel_id=1, replica_groups=mesh['patch'=32,'req'=4,'owner'=2] {'patch','owner'}, use_global_device_ids=true, to_apply=%region_5.6 | all-reduce | flops 64 | bytes 512 | tf_op jit(solution)/shard_map/psum | solution.py:29
  320.5 32.0 %all_gather.14 = bf16[1,2,20480]{2,1,0:T(2,128)(2,1)S(1)} all-gather(bf16[1,2,640]{2,1,0:T(2,128)(2,1)S(1)} %copy-done.16), channel_id=1, replica_groups=mesh['patch'=32,'req'=4,'owner'=2] {'patch'}, dimensions={2}, use_global_device_ids=true | all-gather | bytes 84480 | tf_op jit(solution)/shard_map/all_gather | solution.py:75
  352.5 24.4 %all_gather.15 = bf16[8,2,20480]{2,1,0:T(2,128)(2,1)S(1)} all-gather(bf16[1,2,20480]{2,1,0:T(2,128)(2,1)S(1)} %all_gather.14), channel_id=1, replica_groups=mesh['patch'=32,'req'=4,'owner'=2] {'req','owner'}, dimensions={0}, use_global_device_ids=true | all-gather | bytes 737280 | tf_op jit(solution)/shard_map/all_gather | solution.py:79
  377.0 4.8 slice_bitcast_fusion
  390.1 3.5 collective-permute-start.3
  398.0 5.7 pad_maximum_fusion
  403.7 10.7 %convolution_convert_fusion = bf16[2,2,184320]{2,0,1:T(2,128)(2,1)} fusion(bf16[8,2,184320]{2,1,0:T(2,128)(2,1)} %all-gather.2.cloned.1.call-done, s32[2]{0:T(128)S(1)} %fusion.123), kind=kOutput, calls=%fused_computation | convolution fusion | flops 12533776 | bytes 7372808 | tf_op jit(solution)/shard_map/ik,kjs->ijs/dot_general | solution.py:83
  414.4 4.7 reshape.54
  419.1 3.3 fusion.145
  428.2 2.9 fusion.54
  431.1 2.9 fusion.50
  439.4 2.7 fusion.14
  444.9 9.6 %add_add_fusion.1 = f32[2,8,128,384]{2,3,1,0:T(8,128)} fusion(f32[2,8,128,384]{2,3,1,0:T(8,128)} %fusion.18, f32[2,8,128,384]{2,3,1,0:T(8,128)} %fusion.48, f32[2,8,128,384]{2,3,1,0:T(8,128)} %fusion.50, f32[2,8,128,384]{2,3,1,0:T(8,128)} %fusion.80, f32[2,8,128,384]{2,3,1,0:T(8,128)S(1)} %copy-done.10, f32[2,8,128,384]{2,3,1,0:T(8,128)} %fusion.54, ...), kind=kOutput, calls=%fused_computation.45 | convolution fusion | flops 510590976 | bytes 35520512 | tf_op jit(solution)/shard_map/bhwc,bcd->bhwd/dot_general | solution.py:46
  457.3 122.8 %psum.30 = f32[2,32]{1,0:T(2,128)S(1)} all-reduce(f32[2,32]{1,0:T(2,128)S(1)} %reduce_sum.82), channel_id=1, replica_groups=mesh['patch'=32,'req'=4,'owner'=2] {'patch','owner'}, use_global_device_ids=true, to_apply=%region_9.10 | all-reduce | flops 64 | bytes 512 | tf_op jit(solution)/shard_map/psum | solution.py:26
  581.0 127.5 %psum.31 = f32[2,32]{1,0:T(2,128)S(1)} all-reduce(f32[2,32]{1,0:T(2,128)S(1)} %reduce_sum.85), channel_id=1, replica_groups=mesh['patch'=32,'req'=4,'owner'=2] {'patch','owner'}, use_global_device_ids=true, to_apply=%region_12.13 | all-reduce | flops 64 | bytes 512 | tf_op jit(solution)/shard_map/psum | solution.py:29
  714.9 3.2 fusion.97
  727.7 3.7 collective-permute-start.7
  731.4 4.1 fusion.22
  741.8 5.0 pad_maximum_fusion.1
  752.2 2.9 fusion.40
  755.1 2.9 fusion.36
  760.7 8.9 %add_add_fusion = f32[2,8,128,384]{2,3,1,0:T(8,128)S(1)} fusion(f32[2,8,128,384]{2,3,1,0:T(8,128)} %fusion.26, f32[2,8,128,384]{2,3,1,0:T(8,128)} %fusion.34, f32[2,8,128,384]{2,3,1,0:T(8,128)} %fusion.36, f32[2,8,128,384]{2,3,1,0:T(8,128)S(1)} %copy-done.9, f32[2,8,128,384]{2,3,1,0:T(8,128)} %fusion.38, f32[2,8,128,384]{2,3,1,0:T(8,128)} %fusion.40, ...), kind=kOutput, calls=%fused_computation.44 | convolution fusion | flops 510590976 | bytes 35520512 | tf_op jit(solution)/shard_map/bhwc,bcd->bhwd/dot_general | solution.py:46
  (124 shorter events, 69.0 us)
Async XLA Ops:
  6.5 375.3 %copy-start = (bf16[1280,320]{0,1:T(8,128)(2,1)S(1)}, bf16[1280,320]{0,1:T(8,128)(2,1)}, u32[]{:S(2)}) copy-start(bf16[1280,320]{0,1:T(8,128)(2,1)} %param.12) | copy-start | bytes 2457604
  6.5 184.9 %copy-start.5 = (bf16[2,8,128,320]{2,3,1,0:T(8,128)(2,1)S(1)}, bf16[2,8,128,320]{2,3,1,0:T(8,128)(2,1)}, u32[]{:S(2)}) copy-start(bf16[2,8,128,320]{2,3,1,0:T(8,128)(2,1)} %param.10) | copy-start | bytes 3932164
  6.5 309.9 %copy-start.15 = (f32[2,320]{1,0:T(2,128)S(1)}, f32[2,320]{1,0:T(2,128)}, u32[]{:S(2)}) copy-start(f32[2,320]{1,0:T(2,128)} %param.13) | copy-start | bytes 7684
  6.5 309.9 %copy-start.14 = (f32[2,320]{1,0:T(2,128)S(1)}, f32[2,320]{1,0:T(2,128)}, u32[]{:S(2)}) copy-start(f32[2,320]{1,0:T(2,128)} %param.14) | copy-start | bytes 7684
  6.5 397.2 %all-gather.2.cloned.1.call-start = ((), (), s32[]{:S(2)}) async-start(), calls=%async_computation | async-start | bytes 6635520 | tf_op jit(solution)/shard_map/all_gather | solution.py:78
  53.8 266.6 %copy-start.16 = (bf16[1,2,640]{2,1,0:T(2,128)(2,1)S(1)}, bf16[1,2,640]{2,1,0:T(2,128)(2,1)}, u32[]{:S(2)}) copy-start(bf16[1,2,640]{2,1,0:T(2,128)(2,1)} %param.17) | copy-start | bytes 7684
  317.9 64.4 %collective-permute-start = (bf16[2,1,128,320]{2,3,1,0:T(8,128)(2,1)S(1)}, bf16[2,1,128,320]{2,3,1,0:T(8,128)(2,1)S(1)}, u32[]{:S(2)}, u32[]{:S(2)}) collective-permute-start(bf16[2,1,128,320]{2,3,1,0:T(8,128)(2,1)S(1)} %get-tuple-element.23), channel_id=1, source_target_pairs={{0,8},{8,16},{16,24},{24,32},{32,40},{40,48},{48,56},{56,64},{64,7... | collective-permute-start | bytes 491528 | tf_op jit(solution)/shard_map/ppermute | solution.py:14
  319.2 63.1 %collective-permute-start.1 = (bf16[2,1,128,320]{2,3,1,0:T(8,128)(2,1)S(1)}, bf16[2,1,128,320]{2,3,1,0:T(8,128)(2,1)S(1)}, u32[]{:S(2)}, u32[]{:S(2)}) collective-permute-start(bf16[2,1,128,320]{2,3,1,0:T(8,128)(2,1)S(1)} %get-tuple-element.24), channel_id=1, source_target_pairs={{8,0},{16,8},{24,16},{32,24},{40,32},{48,40},{56,48},{64,56},{72,6... | collective-permute-start | bytes 491528 | tf_op jit(solution)/shard_map/ppermute | solution.py:17
  377.0 5.1 copy-start.17
  377.0 5.1 copy-start.18
  386.9 7.8 collective-permute-start.2
  390.1 6.3 collective-permute-start.3
  708.7 5.5 copy-start.11
  710.1 9.8 %copy-start.3 = (bf16[2,8,128,320]{2,3,1,0:T(8,128)(2,1)}, bf16[2,8,128,320]{2,3,1,0:T(8,128)(2,1)S(1)}, u32[]{:S(2)}) copy-start(bf16[2,8,128,320]{2,3,1,0:T(8,128)(2,1)S(1)} %multiply_convert_fusion) | copy-start | bytes 3932164
  710.2 7.9 %collective-permute-start.4 = (bf16[2,1,128,320]{2,3,1,0:T(8,128)(2,1)S(1)}, bf16[2,1,128,320]{2,3,1,0:T(8,128)(2,1)S(1)}, u32[]{:S(2)}, u32[]{:S(2)}) collective-permute-start(bf16[2,1,128,320]{2,3,1,0:T(8,128)(2,1)S(1)} %get-tuple-element.21), channel_id=1, source_target_pairs={{0,8},{8,16},{16,24},{24,32},{32,40},{40,48},{48,56},{56,64},{64,7... | collective-permute-start | bytes 491528 | tf_op jit(solution)/shard_map/ppermute | solution.py:14
  712.9 7.0 collective-permute-start.5
  724.4 13.8 %collective-permute-start.6 = (bf16[2,10,1,320]{3,0,2,1:T(2,128)(2,1)S(1)}, bf16[2,10,1,320]{3,0,2,1:T(2,128)(2,1)S(1)}, u32[]{:S(2)}, u32[]{:S(2)}) collective-permute-start(bf16[2,10,1,320]{3,0,2,1:T(2,128)(2,1)S(1)} %copy.104), channel_id=1, source_target_pairs={{0,1},{2,3},{4,5},{6,7},{8,9},{10,11},{12,13},{14,15},{16,17},{18,... | collective-permute-start | bytes 38408 | tf_op jit(solution)/shard_map/ppermute | solution.py:14
  725.7 9.8 %slice-start = ((s8[4423680]{0:T(1024)(128)(4,1)}), s8[229376]{0:T(1024)(128)(4,1)S(1)}, s32[]{:S(2)}) async-start(s8[4423680]{0:T(1024)(128)(4,1)} %bitcast.145), calls=%async_computation.1 | async-start | bytes 458752
  727.7 7.8 %slice-start.1 = ((s8[4423680]{0:T(1024)(128)(4,1)}), s8[4194304]{0:T(1024)(128)(4,1)S(1)}, s32[]{:S(2)}) async-start(s8[4423680]{0:T(1024)(128)(4,1)} %bitcast.145), calls=%async_computation.2 | async-start | bytes 8388608
  727.7 7.8 %copy-start.4 = (bf16[2,8,128,320]{2,3,1,0:T(8,128)(2,1)S(1)}, bf16[2,8,128,320]{2,3,1,0:T(8,128)(2,1)}, u32[]{:S(2)}) copy-start(bf16[2,8,128,320]{2,3,1,0:T(8,128)(2,1)} %copy-done.3) | copy-start | bytes 3932164
  727.7 12.5 %collective-permute-start.7 = (bf16[2,10,1,320]{3,0,2,1:T(2,128)(2,1)S(1)}, bf16[2,10,1,320]{3,0,2,1:T(2,128)(2,1)S(1)}, u32[]{:S(2)}, u32[]{:S(2)}) collective-permute-start(bf16[2,10,1,320]{3,0,2,1:T(2,128)(2,1)S(1)} %copy.109), channel_id=1, source_target_pairs={{1,0},{3,2},{5,4},{7,6},{9,8},{11,10},{13,12},{15,14},{17,16},{19,... | collective-permute-start | bytes 38408 | tf_op jit(solution)/shard_map/ppermute | solution.py:17
  740.1 6.7 slice-start.2
  760.7 8.9 %copy-start.6 = (bf16[2,8,128,320]{2,3,1,0:T(8,128)(2,1)S(1)}, bf16[2,8,128,320]{2,3,1,0:T(8,128)(2,1)}, u32[]{:S(2)}) copy-start(bf16[2,8,128,320]{2,3,1,0:T(8,128)(2,1)} %param.10) | copy-start | bytes 3932164
  760.7 10.6 %copy-start.1 = (bf16[1280,320]{0,1:T(8,128)(2,1)S(1)}, bf16[1280,320]{0,1:T(8,128)(2,1)}, u32[]{:S(2)}) copy-start(bf16[1280,320]{0,1:T(8,128)(2,1)} %param.12) | copy-start | bytes 2457604
  (8 other events, 26.5 us)
Sparse Core Ops, SparseCore 0:
  54.0 51.1 all-gather.1
where the time goes:
time: 784 us; the launch traced here: 778 us
  blocking collectives  614 us (78%)
  matrix products  79 us (10%)
  local copies, waits for them, and re-layouts  37.7 us (5%)
  other arithmetic  17 us (2%)
  starting transfers between devices  15 us (2%)
  between operations  14.1 us (2%)
    psum x2, blocking collectives, group_act(): total = lax.psum(jnp.sum(grouped, axis=(1, 2, 4)), ('patch', 'owner'))  258 us
    psum x2, blocking collectives, group_act(): lax.psum(jnp.sum(centered * centered, axis=(1, 2, 4)), ('patch', 'owner'))  252 us
    dot_general x18, matrix products, block_conv(): jnp.einsum('bhwc,bcd->bhwd', window, joined[:, tap], preferred_element_ty...  62.9 us
    all_gather x1, blocking collectives, local(): lax.all_gather(plugin_reduce_library, 'patch', axis=2, tiled=True)  47.2 us
    all_gather x1, blocking collectives, local(): lax.all_gather(plugin_expand_library, 'patch', axis=2, tiled=True)  32 us
    all_gather x1, blocking collectives, local(): lax.all_gather(full_up, ('req', 'owner'), axis=0, tiled=True)  24.4 us
  transfers between devices with their start and end apart: 9, of which 1 were waited for; matrix products, arithmetic and copies ran while one was open for 5% of the time, Pallas kernels for 0%

commit v1 on v0

--- a/solution.py
+++ b/solution.py
@@ -23,7 +23,9 @@
     images, rows, columns, chans = values.shape
     grouped = values.reshape(images, rows, columns, GROUPS, chans // GROUPS)
     count = rows * columns * (chans // GROUPS) * lax.axis_size("patch") * lax.axis_size("owner")
-    total = lax.psum(jnp.sum(grouped, axis=(1, 2, 4)), ("patch", "owner"))
+    total = jnp.sum(grouped, axis=(1, 2, 4))
+    for over in ("patch", "owner"):
+        total = lax.psum(total, over)
     mean = total / count
     centered = grouped - mean[:, None, None, :, None]
     spread = lax.psum(jnp.sum(centered * centered, axis=(1, 2, 4)), ("patch", "owner"))

time: 784 us -> 682 us (0.87)
  blocking collectives: 614 us -> 512 us
    psum x2 -> x4, blocking collectives: 258 us -> 160 us  [group_act(): total = lax.psum(total, over)]
  transfers between devices with their start and end apart: 9 -> 9, of which waited for: 1 -> 1; matrix products, arithmetic and copies ran while one was open for 5% -> 6% of each run, Pallas kernels for 0% -> 0%
where the time goes in v1:
time: 682 us; the launch traced here: 677 us
  blocking collectives  512 us (75%)
  matrix products  79 us (12%)
  local copies, waits for them, and re-layouts  37.7 us (6%)
  other arithmetic  17 us (2%)
  starting transfers between devices  15.2 us (2%)
  between operations  14.1 us (2%)
    psum x2, blocking collectives, group_act(): lax.psum(jnp.sum(centered * centered, axis=(1, 2, 4)), ('patch', 'owner'))  248 us
    psum x4, blocking collectives, group_act(): total = lax.psum(total, over)  160 us
    dot_general x18, matrix products, block_conv(): jnp.einsum('bhwc,bcd->bhwd', window, joined[:, tap], preferred_element_ty...  62.9 us
    all_gather x1, blocking collectives, local(): lax.all_gather(plugin_reduce_library, 'patch', axis=2, tiled=True)  47.2 us
    all_gather x1, blocking collectives, local(): lax.all_gather(plugin_expand_library, 'patch', axis=2, tiled=True)  32 us
    all_gather x1, blocking collectives, local(): lax.all_gather(full_up, ('req', 'owner'), axis=0, tiled=True)  24.6 us
  transfers between devices with their start and end apart: 9, of which 1 were waited for; matrix products, arithmetic and copies ran while one was open for 6% of the time, Pallas kernels for 0%

profile of v1, /device:TPU:1, one launch (start us, length us, event | category | flops | bytes accessed | tf_op | source)
XLA Modules:
  0.0 676.6 jit_solution(5969306463648355335)
XLA Ops:
  6.6 47.2 %all_gather.12 = bf16[1,2,184320]{2,1,0:T(2,128)(2,1)} all-gather(bf16[1,2,5760]{2,1,0:T(2,128)(2,1)} %param.16), channel_id=1, replica_groups=mesh['patch'=32,'req'=4,'owner'=2] {'patch'}, dimensions={2}, use_global_device_ids=true | all-gather | bytes 760320 | tf_op jit(solution)/shard_map/all_gather | solution.py:76
  55.6 58.1 %psum.42 = f32[2,32]{1,0:T(2,128)S(1)} all-reduce(f32[2,32]{1,0:T(2,128)S(1)} %reduce_sum.59), channel_id=1, replica_groups=mesh['patch'=32,'req'=4,'owner'=2] {'patch'}, use_global_device_ids=true, to_apply=%region_2.3 | all-reduce | flops 64 | bytes 512 | tf_op jit(solution)/shard_map/psum | solution.py:28
  113.7 28.6 %psum.43 = f32[2,32]{1,0:T(2,128)S(1)} all-reduce(f32[2,32]{1,0:T(2,128)S(1)} %psum.42), channel_id=1, replica_groups=mesh['patch'=32,'req'=4,'owner'=2] {'owner'}, use_global_device_ids=true, to_apply=%region_3.4 | all-reduce | flops 64 | bytes 512 | tf_op jit(solution)/shard_map/psum | solution.py:28
  143.3 123.7 %psum.44 = f32[2,32]{1,0:T(2,128)S(1)} all-reduce(f32[2,32]{1,0:T(2,128)S(1)} %reduce_sum.62), channel_id=1, replica_groups=mesh['patch'=32,'req'=4,'owner'=2] {'patch','owner'}, use_global_device_ids=true, to_apply=%region_6.7 | all-reduce | flops 64 | bytes 512 | tf_op jit(solution)/shard_map/psum | solution.py:31
  271.3 32.0 %all_gather.14 = bf16[1,2,20480]{2,1,0:T(2,128)(2,1)S(1)} all-gather(bf16[1,2,640]{2,1,0:T(2,128)(2,1)S(1)} %copy-done.16), channel_id=1, replica_groups=mesh['patch'=32,'req'=4,'owner'=2] {'patch'}, dimensions={2}, use_global_device_ids=true | all-gather | bytes 84480 | tf_op jit(solution)/shard_map/all_gather | solution.py:77
  303.3 24.6 %all_gather.15 = bf16[8,2,20480]{2,1,0:T(2,128)(2,1)S(1)} all-gather(bf16[1,2,20480]{2,1,0:T(2,128)(2,1)S(1)} %all_gather.14), channel_id=1, replica_groups=mesh['patch'=32,'req'=4,'owner'=2] {'req','owner'}, dimensions={0}, use_global_device_ids=true | all-gather | bytes 737280 | tf_op jit(solution)/shard_map/all_gather | solution.py:81
  327.9 4.8 slice_bitcast_fusion
  341.0 3.5 collective-permute-start.3
  348.9 5.7 pad_maximum_fusion
  354.7 10.7 %convolution_convert_fusion = bf16[2,2,184320]{2,0,1:T(2,128)(2,1)} fusion(bf16[8,2,184320]{2,1,0:T(2,128)(2,1)} %all-gather.2.cloned.1.call-done, s32[2]{0:T(128)S(1)} %fusion.123), kind=kOutput, calls=%fused_computation | convolution fusion | flops 12533776 | bytes 7372808 | tf_op jit(solution)/shard_map/ik,kjs->ijs/dot_general | solution.py:85
  365.4 4.7 reshape.54
  370.0 3.3 fusion.145
  379.1 2.9 fusion.54
  382.0 2.9 fusion.50
  395.8 9.6 %add_add_fusion.1 = f32[2,8,128,384]{2,3,1,0:T(8,128)} fusion(f32[2,8,128,384]{2,3,1,0:T(8,128)} %fusion.18, f32[2,8,128,384]{2,3,1,0:T(8,128)} %fusion.48, f32[2,8,128,384]{2,3,1,0:T(8,128)} %fusion.50, f32[2,8,128,384]{2,3,1,0:T(8,128)} %fusion.80, f32[2,8,128,384]{2,3,1,0:T(8,128)S(1)} %copy-done.10, f32[2,8,128,384]{2,3,1,0:T(8,128)} %fusion.54, ...), kind=kOutput, calls=%fused_computation.45 | convolution fusion | flops 510590976 | bytes 35520512 | tf_op jit(solution)/shard_map/bhwc,bcd->bhwd/dot_general | solution.py:48
  408.3 58.5 %psum.45 = f32[2,32]{1,0:T(2,128)S(1)} all-reduce(f32[2,32]{1,0:T(2,128)S(1)} %reduce_sum.82), channel_id=1, replica_groups=mesh['patch'=32,'req'=4,'owner'=2] {'patch'}, use_global_device_ids=true, to_apply=%region_10.11 | all-reduce | flops 64 | bytes 512 | tf_op jit(solution)/shard_map/psum | solution.py:28
  466.8 15.1 %psum.46 = f32[2,32]{1,0:T(2,128)S(1)} all-reduce(f32[2,32]{1,0:T(2,128)S(1)} %psum.45), channel_id=1, replica_groups=mesh['patch'=32,'req'=4,'owner'=2] {'owner'}, use_global_device_ids=true, to_apply=%region_11.12 | all-reduce | flops 64 | bytes 512 | tf_op jit(solution)/shard_map/psum | solution.py:28
  482.8 123.9 %psum.47 = f32[2,32]{1,0:T(2,128)S(1)} all-reduce(f32[2,32]{1,0:T(2,128)S(1)} %reduce_sum.85), channel_id=1, replica_groups=mesh['patch'=32,'req'=4,'owner'=2] {'patch','owner'}, use_global_device_ids=true, to_apply=%region_14.15 | all-reduce | flops 64 | bytes 512 | tf_op jit(solution)/shard_map/psum | solution.py:31
  613.1 3.2 fusion.97
  625.7 3.9 collective-permute-start.7
  629.6 4.1 fusion.22
  640.0 5.0 pad_maximum_fusion.1
  650.4 2.9 fusion.40
  658.9 8.9 %add_add_fusion = f32[2,8,128,384]{2,3,1,0:T(8,128)S(1)} fusion(f32[2,8,128,384]{2,3,1,0:T(8,128)} %fusion.26, f32[2,8,128,384]{2,3,1,0:T(8,128)} %fusion.34, f32[2,8,128,384]{2,3,1,0:T(8,128)} %fusion.36, f32[2,8,128,384]{2,3,1,0:T(8,128)S(1)} %copy-done.9, f32[2,8,128,384]{2,3,1,0:T(8,128)} %fusion.38, f32[2,8,128,384]{2,3,1,0:T(8,128)} %fusion.40, ...), kind=kOutput, calls=%fused_computation.44 | convolution fusion | flops 510590976 | bytes 35520512 | tf_op jit(solution)/shard_map/bhwc,bcd->bhwd/dot_general | solution.py:48
  (126 shorter events, 74.4 us)
Async XLA Ops:
  6.5 326.2 %copy-start = (bf16[1280,320]{0,1:T(8,128)(2,1)S(1)}, bf16[1280,320]{0,1:T(8,128)(2,1)}, u32[]{:S(2)}) copy-start(bf16[1280,320]{0,1:T(8,128)(2,1)} %param.12) | copy-start | bytes 2457604
  6.5 136.0 %copy-start.5 = (bf16[2,8,128,320]{2,3,1,0:T(8,128)(2,1)S(1)}, bf16[2,8,128,320]{2,3,1,0:T(8,128)(2,1)}, u32[]{:S(2)}) copy-start(bf16[2,8,128,320]{2,3,1,0:T(8,128)(2,1)} %param.10) | copy-start | bytes 3932164
  6.5 260.7 %copy-start.15 = (f32[2,320]{1,0:T(2,128)S(1)}, f32[2,320]{1,0:T(2,128)}, u32[]{:S(2)}) copy-start(f32[2,320]{1,0:T(2,128)} %param.13) | copy-start | bytes 7684
  6.5 260.7 %copy-start.14 = (f32[2,320]{1,0:T(2,128)S(1)}, f32[2,320]{1,0:T(2,128)}, u32[]{:S(2)}) copy-start(f32[2,320]{1,0:T(2,128)} %param.14) | copy-start | bytes 7684
  6.5 348.1 %all-gather.2.cloned.1.call-start = ((), (), s32[]{:S(2)}) async-start(), calls=%async_computation | async-start | bytes 6635520 | tf_op jit(solution)/shard_map/all_gather | solution.py:80
  53.8 217.4 %copy-start.16 = (bf16[1,2,640]{2,1,0:T(2,128)(2,1)S(1)}, bf16[1,2,640]{2,1,0:T(2,128)(2,1)}, u32[]{:S(2)}) copy-start(bf16[1,2,640]{2,1,0:T(2,128)(2,1)} %param.17) | copy-start | bytes 7684
  268.7 64.6 %collective-permute-start = (bf16[2,1,128,320]{2,3,1,0:T(8,128)(2,1)S(1)}, bf16[2,1,128,320]{2,3,1,0:T(8,128)(2,1)S(1)}, u32[]{:S(2)}, u32[]{:S(2)}) collective-permute-start(bf16[2,1,128,320]{2,3,1,0:T(8,128)(2,1)S(1)} %get-tuple-element.23), channel_id=1, source_target_pairs={{0,8},{8,16},{16,24},{24,32},{32,40},{40,48},{48,56},{56,64},{64,7... | collective-permute-start | bytes 491528 | tf_op jit(solution)/shard_map/ppermute | solution.py:14
  270.0 63.3 %collective-permute-start.1 = (bf16[2,1,128,320]{2,3,1,0:T(8,128)(2,1)S(1)}, bf16[2,1,128,320]{2,3,1,0:T(8,128)(2,1)S(1)}, u32[]{:S(2)}, u32[]{:S(2)}) collective-permute-start(bf16[2,1,128,320]{2,3,1,0:T(8,128)(2,1)S(1)} %get-tuple-element.24), channel_id=1, source_target_pairs={{8,0},{16,8},{24,16},{32,24},{40,32},{48,40},{56,48},{64,56},{72,6... | collective-permute-start | bytes 491528 | tf_op jit(solution)/shard_map/ppermute | solution.py:17
  327.9 5.1 copy-start.17
  327.9 5.1 copy-start.18
  337.8 7.8 %collective-permute-start.2 = (bf16[2,10,1,320]{3,0,2,1:T(2,128)(2,1)S(1)}, bf16[2,10,1,320]{3,0,2,1:T(2,128)(2,1)S(1)}, u32[]{:S(2)}, u32[]{:S(2)}) collective-permute-start(bf16[2,10,1,320]{3,0,2,1:T(2,128)(2,1)S(1)} %copy.87), channel_id=1, source_target_pairs={{0,1},{2,3},{4,5},{6,7},{8,9},{10,11},{12,13},{14,15},{16,17},{18,... | collective-permute-start | bytes 38408 | tf_op jit(solution)/shard_map/ppermute | solution.py:14
  341.0 6.3 collective-permute-start.3
  606.9 5.5 copy-start.11
  608.3 9.6 %copy-start.3 = (bf16[2,8,128,320]{2,3,1,0:T(8,128)(2,1)}, bf16[2,8,128,320]{2,3,1,0:T(8,128)(2,1)S(1)}, u32[]{:S(2)}) copy-start(bf16[2,8,128,320]{2,3,1,0:T(8,128)(2,1)S(1)} %multiply_convert_fusion) | copy-start | bytes 3932164
  608.4 7.9 %collective-permute-start.4 = (bf16[2,1,128,320]{2,3,1,0:T(8,128)(2,1)S(1)}, bf16[2,1,128,320]{2,3,1,0:T(8,128)(2,1)S(1)}, u32[]{:S(2)}, u32[]{:S(2)}) collective-permute-start(bf16[2,1,128,320]{2,3,1,0:T(8,128)(2,1)S(1)} %get-tuple-element.21), channel_id=1, source_target_pairs={{0,8},{8,16},{16,24},{24,32},{32,40},{40,48},{48,56},{56,64},{64,7... | collective-permute-start | bytes 491528 | tf_op jit(solution)/shard_map/ppermute | solution.py:14
  611.2 6.8 %collective-permute-start.5 = (bf16[2,1,128,320]{2,3,1,0:T(8,128)(2,1)S(1)}, bf16[2,1,128,320]{2,3,1,0:T(8,128)(2,1)S(1)}, u32[]{:S(2)}, u32[]{:S(2)}) collective-permute-start(bf16[2,1,128,320]{2,3,1,0:T(8,128)(2,1)S(1)} %get-tuple-element.22), channel_id=1, source_target_pairs={{8,0},{16,8},{24,16},{32,24},{40,32},{48,40},{56,48},{64,56},{72,6... | collective-permute-start | bytes 491528 | tf_op jit(solution)/shard_map/ppermute | solution.py:17
  622.5 14.0 %collective-permute-start.6 = (bf16[2,10,1,320]{3,0,2,1:T(2,128)(2,1)S(1)}, bf16[2,10,1,320]{3,0,2,1:T(2,128)(2,1)S(1)}, u32[]{:S(2)}, u32[]{:S(2)}) collective-permute-start(bf16[2,10,1,320]{3,0,2,1:T(2,128)(2,1)S(1)} %copy.104), channel_id=1, source_target_pairs={{0,1},{2,3},{4,5},{6,7},{8,9},{10,11},{12,13},{14,15},{16,17},{18,... | collective-permute-start | bytes 38408 | tf_op jit(solution)/shard_map/ppermute | solution.py:14
  623.8 9.9 %slice-start = ((s8[4423680]{0:T(1024)(128)(4,1)}), s8[229376]{0:T(1024)(128)(4,1)S(1)}, s32[]{:S(2)}) async-start(s8[4423680]{0:T(1024)(128)(4,1)} %bitcast.145), calls=%async_computation.1 | async-start | bytes 458752
  625.7 8.0 %slice-start.1 = ((s8[4423680]{0:T(1024)(128)(4,1)}), s8[4194304]{0:T(1024)(128)(4,1)S(1)}, s32[]{:S(2)}) async-start(s8[4423680]{0:T(1024)(128)(4,1)} %bitcast.145), calls=%async_computation.2 | async-start | bytes 8388608
  625.7 8.0 %copy-start.4 = (bf16[2,8,128,320]{2,3,1,0:T(8,128)(2,1)S(1)}, bf16[2,8,128,320]{2,3,1,0:T(8,128)(2,1)}, u32[]{:S(2)}) copy-start(bf16[2,8,128,320]{2,3,1,0:T(8,128)(2,1)} %copy-done.3) | copy-start | bytes 3932164
  625.7 12.6 %collective-permute-start.7 = (bf16[2,10,1,320]{3,0,2,1:T(2,128)(2,1)S(1)}, bf16[2,10,1,320]{3,0,2,1:T(2,128)(2,1)S(1)}, u32[]{:S(2)}, u32[]{:S(2)}) collective-permute-start(bf16[2,10,1,320]{3,0,2,1:T(2,128)(2,1)S(1)} %copy.109), channel_id=1, source_target_pairs={{1,0},{3,2},{5,4},{7,6},{9,8},{11,10},{13,12},{15,14},{17,16},{19,... | collective-permute-start | bytes 38408 | tf_op jit(solution)/shard_map/ppermute | solution.py:17
  638.3 6.7 slice-start.2
  658.9 8.9 %copy-start.6 = (bf16[2,8,128,320]{2,3,1,0:T(8,128)(2,1)S(1)}, bf16[2,8,128,320]{2,3,1,0:T(8,128)(2,1)}, u32[]{:S(2)}) copy-start(bf16[2,8,128,320]{2,3,1,0:T(8,128)(2,1)} %param.10) | copy-start | bytes 3932164
  658.9 10.5 %copy-start.1 = (bf16[1280,320]{0,1:T(8,128)(2,1)S(1)}, bf16[1280,320]{0,1:T(8,128)(2,1)}, u32[]{:S(2)}) copy-start(bf16[1280,320]{0,1:T(8,128)(2,1)} %param.12) | copy-start | bytes 2457604
  (8 other events, 26.5 us)
Sparse Core Ops, SparseCore 0:
  54.0 51.1 all-gather.1
